TPU v7x, 128 devices: a whole 4x4x4 slice. The times are simulated.
128 devices in a mesh: row: 8 (over y, z_hi), col: 16 (over x, z_lo, core).
Axes of the slice: x: 4, y: 4, z: 4 (z_hi: 2, z_lo: 2; z = z_hi * 2 + z_lo), core: 2. Of those that a mesh axis runs over, the one named last changes fastest.
Arguments:
- adjacency: bfloat16 [32768, 32768], P('row', 'col'), as said below
- tile_mask: int32 [256, 256], P('row', 'col'), may hold values from 0 to 1, as said below
- out_grad: bfloat16 [32768, 256], P(('row', 'col')), may hold values from -6 to 6
- pre_two: bfloat16 [32768, 256], P(('row', 'col')), may hold values from -6 to 6
- hidden: bfloat16 [32768, 256], P(('col', 'row')), may hold values from -24 to 24
- pre_one: bfloat16 [32768, 256], P(('col', 'row')), may hold values from -6 to 6
- features: bfloat16 [32768, 256], P(('row', 'col')), may hold values from -6 to 6
- w_two: bfloat16 [256, 256], replicated, may hold values from -0.375 to 0.375
- w_one: bfloat16 [256, 256], replicated, may hold values from -0.375 to 0.375
Outputs:
- node_grad: bfloat16 [32768, 256], P(('row', 'col'))
- weight_grad_one: float32 [256, 256], replicated
- weight_grad_two: float32 [256, 256], replicated
Inputs may be any that keep to these rules, and one draw needn't show every extreme that they name: adjacency is symmetric and nonnegative. tile_mask is symmetric and every diagonal tile is 1.
All inputs are finite; a program needn't handle non-finite values.
Results may differ from a plain program's by a relative error of at most 0.02.
Values may be sent and summed in bfloat16 or wider, within the bound.
A program may use at most 128 MiB of HBM per device.

v0:
```python
import jax
import jax.numpy as jnp
from jax import lax
from jax.sharding import PartitionSpec as P


def tile_pick(count, tile_size, tile_total):
    node_ids = lax.broadcasted_iota(jnp.int32, (count, 1), 0)
    tile_ids = lax.broadcasted_iota(jnp.int32, (1, tile_total), 1)
    return (node_ids // tile_size == tile_ids).astype(jnp.bfloat16)


def local(adjacency, tile_mask, out_grad, pre_two, hidden, pre_one, features, w_two, w_one):
    tile_rows, tile_cols = tile_mask.shape
    tile_size = adjacency.shape[0] // tile_rows
    mask_values = tile_mask.astype(jnp.bfloat16)
    shard_nodes = out_grad.shape[0]
    weight_scale = 4.0 * shard_nodes ** (-0.5)
    contract_rows = (((0,), (0,)), ((), ()))
    contract_cols = (((1,), (1,)), ((), ()))
    grad_two = jnp.where(pre_two > 0, out_grad, jnp.zeros_like(out_grad))
    shard_rows = lax.all_gather(grad_two, "col", axis=0, tiled=True)
    count = shard_rows.shape[0]
    strip_rows = adjacency
    picker = tile_pick(count, tile_size, tile_rows)
    strip_mask = jnp.dot(picker, mask_values, preferred_element_type=jnp.float32).astype(
        jnp.bfloat16
    )
    strip_rows = (strip_rows.reshape(count, tile_cols, tile_size) * strip_mask[:, :, None]).reshape(
        count, adjacency.shape[1]
    )
    column_part = lax.dot_general(
        strip_rows, shard_rows, contract_rows, preferred_element_type=jnp.float32
    )
    column_part = column_part.astype(jnp.bfloat16).astype(jnp.float32)
    prop_two = lax.psum_scatter(
        column_part.astype(jnp.bfloat16), "row", scatter_dimension=0, tiled=True
    )
    back_grad = lax.dot_general(prop_two, w_two, contract_cols, preferred_element_type=jnp.float32)
    grad_one = jnp.where(pre_one > 0, back_grad, jnp.zeros_like(back_grad)).astype(jnp.bfloat16)
    shard_rows = lax.all_gather(grad_one, "row", axis=0, tiled=True)
    count = shard_rows.shape[0]
    strip_cols = adjacency
    picker = tile_pick(count, tile_size, tile_cols)
    strip_mask = lax.dot_general(
        mask_values, picker, contract_cols, preferred_element_type=jnp.float32
    ).astype(jnp.bfloat16)
    strip_cols = (strip_cols.reshape(tile_rows, tile_size, count) * strip_mask[:, None, :]).reshape(
        adjacency.shape[0], count
    )
    row_part = jnp.dot(strip_cols, shard_rows, preferred_element_type=jnp.float32)
    term_two = lax.dot_general(hidden, prop_two, contract_rows, preferred_element_type=jnp.float32)
    summed_two = lax.psum(term_two, ("row", "col"))
    row_part = row_part.astype(jnp.bfloat16).astype(jnp.float32)
    prop_one = lax.psum_scatter(
        row_part.astype(jnp.bfloat16), "col", scatter_dimension=0, tiled=True
    )
    term_one = lax.dot_general(
        features, prop_one, contract_rows, preferred_element_type=jnp.float32
    )
    node_grad = lax.dot_general(
        prop_one, w_one, contract_cols, preferred_element_type=jnp.float32
    ).astype(jnp.bfloat16)
    summed_one = lax.psum(term_one, ("row", "col"))
    return (node_grad, summed_one * weight_scale, summed_two * weight_scale)


def solution(mesh):
    return jax.shard_map(
        local,
        mesh=mesh,
        in_specs=(
            P("row", "col"),
            P("row", "col"),
            P(("row", "col"), None),
            P(("row", "col"), None),
            P(("col", "row"), None),
            P(("col", "row"), None),
            P(("row", "col"), None),
            P(),
            P(),
        ),
        out_specs=(P(("row", "col"), None), P(), P()),
        check_vma=False,
    )
```

profile of v0, /device:TPU:1, one launch (start us, length us, event | category | flops | bytes accessed | tf_op | source)
XLA Modules:
  0.0 437.8 jit_solution(10373811274106707431)
XLA Ops:
  7.2 1.7 compare_select_fusion
  8.9 0.0 reduce-scatter.3.cloned.1.call-start
  9.0 0.9 convolution_convert_fusion.1
  9.9 0.5 copy.15
  10.4 37.4 %all-gather.3.cloned.1.call-done = bf16[4096,256]{1,0:T(8,128)(2,1)} async-done(((bf16[256,256]{1,0:T(8,128)(2,1)}), bf16[4096,256]{1,0:T(8,128)(2,1)}) %all-gather.3.cloned.1.call-update) | async-done | bytes 2097168 | tf_op jit(solution)/shard_map/all_gather | solution.py:22
  47.7 18.8 %mul.31 = bf16[4096,16,128]{2,1,0:T(8,128)(2,1)} broadcast(bf16[4096,16]{1,0:T(8,128)(2,1)S(1)} %copy.15), dimensions={0,1} | broadcast | bytes 16908288 | tf_op jit(solution)/shard_map/mul | solution.py:29
  66.5 14.3 %fusion.2 = bf16[2048,256]{1,0:T(8,128)(2,1)} fusion(bf16[4096,256]{1,0:T(8,128)(2,1)S(1)} %copy-done.7, bf16[4096,2048]{1,0:T(8,128)(2,1)} %param.9, bf16[512,8,16,128]{3,2,1,0:T(8,128)(2,1)} %bitcast.25), kind=kOutput, calls=%fused_computation.6 | convolution fusion | flops 4303880192 | bytes 36700160 | tf_op jit(solution)/shard_map/dot_general | solution.py:32
  80.9 0.0 all-gather.5.cloned.1.call-start
  80.9 70.7 %reduce-scatter.3.cloned.1.call-done = bf16[256,256]{1,0:T(8,128)(2,1)} async-done(((bf16[2048,256]{1,0:T(8,128)(2,1)}), bf16[256,256]{1,0:T(8,128)(2,1)}) %reduce-scatter.3.cloned.1.call-update) | async-done | bytes 131088 | tf_op jit(solution)/shard_map/reduce_scatter | solution.py:36
  151.6 1.8 fusion.4
  153.4 0.0 reduce-scatter.5.cloned.1.call-start
  153.5 0.5 fusion.3
  154.0 13.9 %bitcast_multiply_fusion.2 = bf16[4096,2048]{1,0:T(8,128)(2,1)} fusion(bf16[4096,2048]{1,0:T(8,128)(2,1)} %param.9, bf16[32,2048]{1,0:T(8,128)(2,1)S(1)} %fusion.3), kind=kLoop, calls=%fused_computation.3 | loop fusion | flops 8388608 | bytes 33685504 | tf_op jit(solution)/shard_map/mul | solution.py:48
  167.9 33.0 %all-gather.5.cloned.1.call-done = bf16[2048,256]{1,0:T(8,128)(2,1)} async-done(((bf16[256,256]{1,0:T(8,128)(2,1)}), bf16[2048,256]{1,0:T(8,128)(2,1)}) %all-gather.5.cloned.1.call-update) | async-done | bytes 1048592 | tf_op jit(solution)/shard_map/all_gather | solution.py:41
  201.0 11.9 %convolution_convert_fusion = bf16[4096,256]{1,0:T(8,128)(2,1)} fusion(bf16[4096,2048]{1,0:T(8,128)(2,1)} %bitcast_multiply_fusion.2, bf16[2048,256]{1,0:T(8,128)(2,1)} %all-gather.5.cloned.1.call-done), kind=kOutput, calls=%fused_computation.4 | convolution fusion | flops 4296015872 | bytes 19922944 | tf_op jit(solution)/shard_map/dot_general | solution.py:51
  212.9 0.0 all-reduce.3.cloned.1.call-start
  213.0 0.9 convolution_bitcast_fusion
  213.9 60.4 %reduce-scatter.5.cloned.1.call-done = bf16[256,256]{1,0:T(8,128)(2,1)} async-done(((bf16[4096,256]{1,0:T(8,128)(2,1)}), bf16[256,256]{1,0:T(8,128)(2,1)}) %reduce-scatter.5.cloned.1.call-update) | async-done | bytes 131088 | tf_op jit(solution)/shard_map/reduce_scatter | solution.py:55
  274.3 1.8 convolution_bitcast_fusion.1
  276.2 1.8 convolution_convert_fusion.3
  278.0 150.5 %all-reduce.3.cloned.1.call-done = (f32[256,256]{0,1:T(8,128)}, f32[256,256]{0,1:T(8,128)}) async-done(((f32[256,256]{0,1:T(8,128)}, f32[256,256]{0,1:T(8,128)}), (f32[256,256]{0,1:T(8,128)}, f32[256,256]{0,1:T(8,128)})) %all-reduce.3.cloned.1.call-update) | async-done | bytes 524304 | tf_op jit(solution)/shard_map/psum | solution.py:64
  428.5 1.1 broadcast_multiply_fusion
  429.6 0.8 copy.16
  430.4 0.8 copy.17
  (24 shorter events, 0.2 us)
Async XLA Ops:
  7.2 144.5 %copy-start = (bf16[256,256]{1,0:T(8,128)(2,1)S(1)}, bf16[256,256]{1,0:T(8,128)(2,1)}, u32[]{:S(2)}) copy-start(bf16[256,256]{1,0:T(8,128)(2,1)} %param.16) | copy-start | bytes 393220
  7.2 40.5 %all-gather.3.cloned.1.call-start = ((), (), s32[]{:S(2)}) async-start(), calls=%async_computation.2 | async-start | bytes 2228224 | tf_op jit(solution)/shard_map/all_gather | solution.py:22
  8.9 142.7 %reduce-scatter.3.cloned.1.call-start = ((), (), s32[]{:S(2)}) async-start(), calls=%async_computation.3 | async-start | bytes 1179648 | tf_op jit(solution)/shard_map/reduce_scatter | solution.py:36
  47.7 18.8 %copy-start.7 = (bf16[4096,256]{1,0:T(8,128)(2,1)S(1)}, bf16[4096,256]{1,0:T(8,128)(2,1)}, u32[]{:S(2)}) copy-start(bf16[4096,256]{1,0:T(8,128)(2,1)} %all-gather.3.cloned.1.call-done) | copy-start | bytes 6291460
  66.5 85.1 %copy-start.3 = (bf16[256,256]{1,0:T(8,128)(2,1)S(1)}, bf16[256,256]{1,0:T(8,128)(2,1)}, u32[]{:S(2)}) copy-start(bf16[256,256]{1,0:T(8,128)(2,1)} %param.14) | copy-start | bytes 393220
  66.5 87.0 %copy-start.6 = (s32[32,16]{0,1:T(8,128)S(1)}, s32[32,16]{0,1:T(8,128)}, u32[]{:S(2)}) copy-start(s32[32,16]{0,1:T(8,128)} %param.10) | copy-start | bytes 6148
  80.9 120.1 %all-gather.5.cloned.1.call-start = ((), (), s32[]{:S(2)}) async-start(), calls=%async_computation.4 | async-start | bytes 1179648 | tf_op jit(solution)/shard_map/all_gather | solution.py:41
  153.4 120.9 %reduce-scatter.5.cloned.1.call-start = ((), (), s32[]{:S(2)}) async-start(), calls=%async_computation.5 | async-start | bytes 2228224 | tf_op jit(solution)/shard_map/reduce_scatter | solution.py:55
  167.9 45.0 %copy-start.1 = (bf16[256,256]{1,0:T(8,128)(2,1)S(1)}, bf16[256,256]{1,0:T(8,128)(2,1)}, u32[]{:S(2)}) copy-start(bf16[256,256]{1,0:T(8,128)(2,1)} %reduce-scatter.3.cloned.1.call-done) | copy-start | bytes 393220
  167.9 45.0 %copy-start.4 = (bf16[256,256]{1,0:T(8,128)(2,1)S(1)}, bf16[256,256]{1,0:T(8,128)(2,1)}, u32[]{:S(2)}) copy-start(bf16[256,256]{1,0:T(8,128)(2,1)} %param.13) | copy-start | bytes 393220
  167.9 106.4 %copy-start.5 = (bf16[256,256]{1,0:T(8,128)(2,1)S(1)}, bf16[256,256]{1,0:T(8,128)(2,1)}, u32[]{:S(2)}) copy-start(bf16[256,256]{1,0:T(8,128)(2,1)} %param.15) | copy-start | bytes 393220
  167.9 108.2 %copy-start.2 = (bf16[256,256]{1,0:T(8,128)(2,1)S(1)}, bf16[256,256]{1,0:T(8,128)(2,1)}, u32[]{:S(2)}) copy-start(bf16[256,256]{1,0:T(8,128)(2,1)} %param.17) | copy-start | bytes 393220
  212.9 215.6 %all-reduce.3.cloned.1.call-start = ((), (), s32[]{:S(2)}) async-start(), calls=%async_computation.6 | async-start | bytes 1048576 | tf_op jit(solution)/shard_map/psum | solution.py:64
Sparse Core Ops, SparseCore 0:
  10.3 37.4 all-gather.2
  81.0 70.5 reduce-scatter.2
  154.5 46.3 all-gather.4
  213.0 61.2 reduce-scatter.4
  279.7 148.7 all-reduce.2
where the time goes:
time: 438 us
  waiting for transfers between devices  352 us (80%)
  matrix products  33.9 us (8%)
  local copies, waits for them, and re-layouts  21 us (5%)
  other arithmetic  16.7 us (4%)
  between operations  13.9 us (3%)
    psum x1, waiting for transfers between devices, local(): summed_one = lax.psum(term_one, ('row', 'col'))  151 us
    reduce_scatter x1, waiting for transfers between devices, local(): lax.psum_scatter(column_part.astype(jnp.bfloat16), 'row', scatter_dimensi...  70.7 us
    reduce_scatter x1, waiting for transfers between devices, local(): lax.psum_scatter(row_part.astype(jnp.bfloat16), 'col', scatter_dimension=...  60.4 us
    all_gather x1, waiting for transfers between devices, local(): shard_rows = lax.all_gather(grad_two, 'col', axis=0, tiled=True)  37.4 us
    all_gather x1, waiting for transfers between devices, local(): shard_rows = lax.all_gather(grad_one, 'row', axis=0, tiled=True)  33 us
    mul x1, local copies, waits for them, and re-layouts, local(): strip_rows.reshape(count, tile_cols, tile_size) * strip_mask[:, :, None]  18.8 us
    dot_general x1, matrix products, local(): lax.dot_general(strip_rows, shard_rows, contract_rows, preferred_element_...  14.3 us
    mul x1, other arithmetic, local(): strip_cols.reshape(tile_rows, tile_size, count) * strip_mask[:, None, :]  13.9 us
  transfers between devices with their start and end apart: 5, of which 5 were waited for; matrix products, arithmetic and copies ran while one was open for 4% of the time, Pallas kernels for 0%

commit v1 on v0

--- a/solution.py
+++ b/solution.py
@@ -61,7 +61,8 @@
     node_grad = lax.dot_general(
         prop_one, w_one, contract_cols, preferred_element_type=jnp.float32
     ).astype(jnp.bfloat16)
-    summed_one = lax.psum(term_one, ("row", "col"))
+    parts = lax.all_gather(term_one, ("row", "col"), axis=0, tiled=False)
+    summed_one = parts.sum(axis=0)
     return (node_grad, summed_one * weight_scale, summed_two * weight_scale)
 
 

time: 438 us -> 690 us (1.58)
  waiting for transfers between devices: 352 us -> 579 us
  local copies, waits for them, and re-layouts: 21 us -> 40.6 us
    all_gather x0 -> x1, waiting for transfers between devices: none -> 230 us  [local(): parts = lax.all_gather(term_one, ('row', 'col'), axis=0, tiled=False)]
    unnamed x18 -> x21, local copies, waits for them, and re-layouts: 1.71 us -> 21.3 us
  transfers between devices with their start and end apart: 5 -> 6, of which waited for: 5 -> 6; matrix products, arithmetic and copies ran while one was open for 4% -> 3% of each run, Pallas kernels for 0% -> 0%
where the time goes in v1:
time: 690 us; the launch traced here: 689 us
  waiting for transfers between devices  579 us (84%)
  local copies, waits for them, and re-layouts  40.6 us (6%)
  matrix products  33.9 us (5%)
  other arithmetic  20.7 us (3%)
  between operations  14.2 us (2%)
    all_gather x1, waiting for transfers between devices, local(): parts = lax.all_gather(term_one, ('row', 'col'), axis=0, tiled=False)  230 us
    psum x1, waiting for transfers between devices, local(): summed_two = lax.psum(term_two, ('row', 'col'))  148 us
    reduce_scatter x1, waiting for transfers between devices, local(): lax.psum_scatter(column_part.astype(jnp.bfloat16), 'row', scatter_dimensi...  70.7 us
    reduce_scatter x1, waiting for transfers between devices, local(): lax.psum_scatter(row_part.astype(jnp.bfloat16), 'col', scatter_dimension=...  60.3 us
    all_gather x1, waiting for transfers between devices, local(): shard_rows = lax.all_gather(grad_two, 'col', axis=0, tiled=True)  37.4 us
    all_gather x1, waiting for transfers between devices, local(): shard_rows = lax.all_gather(grad_one, 'row', axis=0, tiled=True)  33.1 us
    unnamed x21, local copies, waits for them, and re-layouts  21.3 us
    mul x1, local copies, waits for them, and re-layouts, local(): strip_rows.reshape(count, tile_cols, tile_size) * strip_mask[:, :, None]  18.8 us
  transfers between devices with their start and end apart: 6, of which 6 were waited for; matrix products, arithmetic and copies ran while one was open for 3% of the time, Pallas kernels for 0%

profile of v1, /device:TPU:1, one launch (start us, length us, event | category | flops | bytes accessed | tf_op | source)
XLA Modules:
  0.0 689.2 jit_solution(14412068116893561795)
XLA Ops:
  7.2 1.7 compare_select_fusion
  9.0 0.9 convolution_convert_fusion.1
  9.9 0.5 copy.15
  10.4 37.4 %all-gather.5.cloned.1.call-done = bf16[4096,256]{1,0:T(8,128)(2,1)} async-done(((bf16[256,256]{1,0:T(8,128)(2,1)}), bf16[4096,256]{1,0:T(8,128)(2,1)}) %all-gather.5.cloned.1.call-update) | async-done | bytes 2097168 | tf_op jit(solution)/shard_map/all_gather | solution.py:22
  47.7 18.8 %mul.31 = bf16[4096,16,128]{2,1,0:T(8,128)(2,1)} broadcast(bf16[4096,16]{1,0:T(8,128)(2,1)S(1)} %copy.15), dimensions={0,1} | broadcast | bytes 16908288 | tf_op jit(solution)/shard_map/mul | solution.py:29
  66.5 14.3 %fusion.2 = bf16[2048,256]{1,0:T(8,128)(2,1)} fusion(bf16[4096,256]{1,0:T(8,128)(2,1)S(1)} %copy-done.8, bf16[4096,2048]{1,0:T(8,128)(2,1)} %param.9, bf16[512,8,16,128]{3,2,1,0:T(8,128)(2,1)} %bitcast.31), kind=kOutput, calls=%fused_computation.7 | convolution fusion | flops 4303880192 | bytes 36700160 | tf_op jit(solution)/shard_map/dot_general | solution.py:32
  80.9 70.7 %reduce-scatter.3.cloned.1.call-done = bf16[256,256]{1,0:T(8,128)(2,1)} async-done(((bf16[2048,256]{1,0:T(8,128)(2,1)}), bf16[256,256]{1,0:T(8,128)(2,1)}) %reduce-scatter.3.cloned.1.call-update) | async-done | bytes 131088 | tf_op jit(solution)/shard_map/reduce_scatter | solution.py:36
  151.6 1.8 fusion.4
  153.5 0.5 fusion.3
  154.0 13.9 %bitcast_multiply_fusion.2 = bf16[4096,2048]{1,0:T(8,128)(2,1)} fusion(bf16[4096,2048]{1,0:T(8,128)(2,1)} %param.9, bf16[32,2048]{1,0:T(8,128)(2,1)S(1)} %fusion.3), kind=kLoop, calls=%fused_computation.4 | loop fusion | flops 8388608 | bytes 33685504 | tf_op jit(solution)/shard_map/mul | solution.py:48
  167.9 33.1 %all-gather.7.cloned.1.call-done = bf16[2048,256]{1,0:T(8,128)(2,1)} async-done(((bf16[256,256]{1,0:T(8,128)(2,1)}), bf16[2048,256]{1,0:T(8,128)(2,1)}) %all-gather.7.cloned.1.call-update) | async-done | bytes 1048592 | tf_op jit(solution)/shard_map/all_gather | solution.py:41
  201.0 11.9 %convolution_convert_fusion = bf16[4096,256]{1,0:T(8,128)(2,1)} fusion(bf16[4096,2048]{1,0:T(8,128)(2,1)} %bitcast_multiply_fusion.2, bf16[2048,256]{1,0:T(8,128)(2,1)} %all-gather.7.cloned.1.call-done), kind=kOutput, calls=%fused_computation.5 | convolution fusion | flops 4296015872 | bytes 19922944 | tf_op jit(solution)/shard_map/dot_general | solution.py:51
  212.9 0.9 convolution_bitcast_fusion
  213.9 0.2 all-gather.9.cloned.1.call-start
  214.1 60.3 %reduce-scatter.5.cloned.1.call-done = bf16[256,256]{1,0:T(8,128)(2,1)} async-done(((bf16[4096,256]{1,0:T(8,128)(2,1)}), bf16[256,256]{1,0:T(8,128)(2,1)}) %reduce-scatter.5.cloned.1.call-update) | async-done | bytes 131088 | tf_op jit(solution)/shard_map/reduce_scatter | solution.py:55
  274.4 1.8 convolution_bitcast_fusion.1
  276.3 148.3 %all-reduce.2.cloned.1.call-done = f32[256,256]{0,1:T(8,128)} async-done(((f32[256,256]{0,1:T(8,128)}), f32[256,256]{0,1:T(8,128)}) %all-reduce.2.cloned.1.call-update) | async-done | bytes 262160 | tf_op jit(solution)/shard_map/psum | solution.py:53
  424.6 1.0 broadcast_multiply_fusion
  425.5 0.8 copy.17
  426.4 1.8 convolution_convert_fusion.3
  428.1 229.6 %all-gather.9.cloned.1.call-done = f32[32768,256]{0,1:T(8,128)} async-done(((f32[256,256]{0,1:T(8,128)}), f32[32768,256]{0,1:T(8,128)}) %all-gather.9.cloned.1.call-update) | async-done | bytes 33554448 | tf_op jit(solution)/shard_map/all_gather | solution.py:64
  657.7 19.6 %copy.19 = f32[32,8,128,256]{3,2,1,0:T(8,128)S(1)} copy(f32[32,8,128,256]{3,1,2,0:T(8,128)} %bitcast.30) | data formatting | bytes 67108864
  677.4 4.1 bitcast_reduce_fusion
  681.5 0.8 copy.16
  (32 shorter events, 0.4 us)
Async XLA Ops:
  7.2 144.4 %copy-start = (bf16[256,256]{1,0:T(8,128)(2,1)S(1)}, bf16[256,256]{1,0:T(8,128)(2,1)}, u32[]{:S(2)}) copy-start(bf16[256,256]{1,0:T(8,128)(2,1)} %param.16) | copy-start | bytes 393220
  7.2 40.5 %all-gather.5.cloned.1.call-start = ((), (), s32[]{:S(2)}) async-start(), calls=%async_computation.2 | async-start | bytes 2228224 | tf_op jit(solution)/shard_map/all_gather | solution.py:22
  8.9 142.7 %reduce-scatter.3.cloned.1.call-start = ((), (), s32[]{:S(2)}) async-start(), calls=%async_computation.3 | async-start | bytes 1179648 | tf_op jit(solution)/shard_map/reduce_scatter | solution.py:36
  47.7 18.8 %copy-start.8 = (bf16[4096,256]{1,0:T(8,128)(2,1)S(1)}, bf16[4096,256]{1,0:T(8,128)(2,1)}, u32[]{:S(2)}) copy-start(bf16[4096,256]{1,0:T(8,128)(2,1)} %all-gather.5.cloned.1.call-done) | copy-start | bytes 6291460
  66.5 85.1 %copy-start.4 = (bf16[256,256]{1,0:T(8,128)(2,1)S(1)}, bf16[256,256]{1,0:T(8,128)(2,1)}, u32[]{:S(2)}) copy-start(bf16[256,256]{1,0:T(8,128)(2,1)} %param.14) | copy-start | bytes 393220
  66.5 87.0 %copy-start.7 = (s32[32,16]{0,1:T(8,128)S(1)}, s32[32,16]{0,1:T(8,128)}, u32[]{:S(2)}) copy-start(s32[32,16]{0,1:T(8,128)} %param.10) | copy-start | bytes 6148
  80.9 120.1 %all-gather.7.cloned.1.call-start = ((), (), s32[]{:S(2)}) async-start(), calls=%async_computation.4 | async-start | bytes 1179648 | tf_op jit(solution)/shard_map/all_gather | solution.py:41
  153.4 121.0 %reduce-scatter.5.cloned.1.call-start = ((), (), s32[]{:S(2)}) async-start(), calls=%async_computation.5 | async-start | bytes 2228224 | tf_op jit(solution)/shard_map/reduce_scatter | solution.py:55
  167.9 45.0 %copy-start.2 = (bf16[256,256]{1,0:T(8,128)(2,1)S(1)}, bf16[256,256]{1,0:T(8,128)(2,1)}, u32[]{:S(2)}) copy-start(bf16[256,256]{1,0:T(8,128)(2,1)} %reduce-scatter.3.cloned.1.call-done) | copy-start | bytes 393220
  167.9 45.0 %copy-start.5 = (bf16[256,256]{1,0:T(8,128)(2,1)S(1)}, bf16[256,256]{1,0:T(8,128)(2,1)}, u32[]{:S(2)}) copy-start(bf16[256,256]{1,0:T(8,128)(2,1)} %param.13) | copy-start | bytes 393220
  167.9 106.5 %copy-start.6 = (bf16[256,256]{1,0:T(8,128)(2,1)S(1)}, bf16[256,256]{1,0:T(8,128)(2,1)}, u32[]{:S(2)}) copy-start(bf16[256,256]{1,0:T(8,128)(2,1)} %param.15) | copy-start | bytes 393220
  167.9 258.5 %copy-start.3 = (bf16[256,256]{1,0:T(8,128)(2,1)S(1)}, bf16[256,256]{1,0:T(8,128)(2,1)}, u32[]{:S(2)}) copy-start(bf16[256,256]{1,0:T(8,128)(2,1)} %param.17) | copy-start | bytes 393220
  212.9 211.7 %all-reduce.2.cloned.1.call-start = ((), (), s32[]{:S(2)}) async-start(), calls=%async_computation.6 | async-start | bytes 524288 | tf_op jit(solution)/shard_map/psum | solution.py:53
  213.9 443.9 %all-gather.9.cloned.1.call-start = ((), (), s32[]{:S(2)}) async-start(), calls=%async_computation.7 | async-start | bytes 33816576 | tf_op jit(solution)/shard_map/all_gather | solution.py:64
  657.7 24.6 %copy-start.1 = (bf16[256,256]{1,0:T(8,128)(2,1)S(1)}, bf16[256,256]{1,0:T(8,128)(2,1)}, u32[]{:S(2)}) copy-start(bf16[256,256]{1,0:T(8,128)(2,1)} %param.16) | copy-start | bytes 393220
Sparse Core Ops, SparseCore 0:
  10.3 37.4 all-gather.4
  81.0 70.5 reduce-scatter.2
  154.5 46.3 all-gather.6
  213.0 61.4 reduce-scatter.4
  279.6 144.9 all-reduce.1
  426.7 230.9 all-gather.8
